TPU v7x, 32 devices: a whole 2x2x4 slice. The times are simulated.
32 devices in a mesh: trow: 4 (over y, core), tcol: 8 (over z, x).
Axes of the slice: x: 2, y: 2, z: 4, core: 2. Of those that a mesh axis runs over, the one named last changes fastest.
Arguments:
- response: bfloat16 [4096, 16384], P('trow', 'tcol'), may hold values from -0.046875 to 0.046875
- test_matrix: bfloat16 [1024, 192], P(('trow', 'tcol')), may hold values from -6 to 6
- slopes: bfloat16 [16384, 256], P('tcol', 'trow'), may hold values from -6 to 6
- ranks: int32 [4, 16], P('trow', 'tcol'), may hold values from 16 to 192, as said below
Outputs:
- commands: float32 [4096, 256], P(('trow', 'tcol'))
Inputs may be any that keep to these rules, and one draw needn't show every extreme that they name: ranks of tiles near the diagonal tend to be higher, and every tile's sketch has full column rank and is well conditioned.
All inputs are finite; a program needn't handle non-finite values.
Results may differ from a plain program's by a relative error of at most 0.014.
Values may be sent and summed in bfloat16 or wider, within the bound.
A program may use at most 64 MiB of HBM per device.

v0:
```python
import jax
import jax.numpy as jnp
from jax import lax
from jax.sharding import PartitionSpec as P


def fetch_frames(slopes):
    return lax.all_gather(slopes, "trow", axis=1, tiled=True)


def on_device(response, test_matrix, slopes, ranks):
    highest = lax.Precision.HIGHEST
    tile_rows = ranks.shape[0]
    tile_cols = ranks.shape[1]
    width = response.shape[0] // tile_rows
    sketch_width = test_matrix.shape[1]
    tiles = response.reshape(tile_rows, width, tile_cols, width)
    row_block = lax.all_gather(test_matrix, "tcol", axis=0, tiled=True)
    sketch = jnp.einsum(
        "rick,kj->rcij",
        tiles,
        lax.all_gather(row_block, "trow", axis=0, tiled=True),
        preferred_element_type=jnp.float32,
    )
    gram = jnp.einsum("rcik,rcil->rckl", sketch, sketch, precision=highest)
    chol = jnp.linalg.cholesky(gram)
    basis = jax.scipy.linalg.solve_triangular(chol, jnp.swapaxes(sketch, 2, 3), lower=True)
    slots = jnp.arange(sketch_width, dtype=jnp.int32)
    keep = (slots[None, None, :] < ranks[:, :, None]).astype(jnp.float32)
    basis = (basis * keep[:, :, :, None]).astype(jnp.bfloat16)
    factor = jnp.einsum("rcsi,ricj->rcsj", basis, tiles, preferred_element_type=jnp.float32).astype(
        jnp.bfloat16
    )
    frames = fetch_frames(slopes)
    frame_count = frames.shape[1]
    frame_tiles = frames.reshape(tile_cols, width, frame_count)
    coeff = jnp.einsum(
        "rcsj,cjf->rcsf", factor, frame_tiles, preferred_element_type=jnp.float32
    ).astype(jnp.bfloat16)
    share_rows = tile_rows * width // lax.axis_size("tcol")
    summed = jnp.einsum("rcsi,rcsf->rif", basis, coeff, preferred_element_type=jnp.float32)
    summed_all = lax.psum(
        summed.reshape(tile_rows * width, frame_count).astype(jnp.bfloat16), "tcol"
    ).astype(jnp.float32)
    result = lax.dynamic_slice_in_dim(
        summed_all, lax.axis_index("tcol") * share_rows, share_rows, 0
    )
    return result


def solution(mesh):
    return jax.shard_map(
        on_device,
        mesh=mesh,
        in_specs=(
            P("trow", "tcol"),
            P(("trow", "tcol"), None),
            P("tcol", "trow"),
            P("trow", "tcol"),
        ),
        out_specs=P(("trow", "tcol"), None),
        check_vma=False,
    )
```

profile of v0, /device:TPU:0, one launch (start us, length us, event | category | flops | bytes accessed | tf_op | source)
XLA Modules:
  0.0 238.7 jit_solution(7302587469162838817)
XLA Ops:
  6.5 0.0 all-gather.2.cloned.1.call-start
  6.5 0.7 all-gather.2.cloned.1.call-update
  7.3 0.0 all-reduce.5.cloned.1.call-start
  7.4 32.5 %all_gather.9 = bf16[256,192]{1,0:T(8,128)(2,1)S(1)} all-gather(bf16[32,192]{1,0:T(8,128)(2,1)} %param.5), channel_id=1, replica_groups=mesh['trow'=4,'tcol'=8] {'tcol'}, dimensions={0}, use_global_device_ids=true | all-gather | bytes 110592 | tf_op jit(solution)/shard_map/all_gather | solution.py:18
  39.9 0.1 copy.21
  40.1 6.5 %all_gather.10 = bf16[1024,192]{0,1:T(8,128)(2,1)S(1)} all-gather(bf16[256,192]{0,1:T(8,128)(2,1)S(1)} %copy.21), channel_id=1, replica_groups=mesh['trow'=4,'tcol'=8] {'trow'}, dimensions={0}, use_global_device_ids=true | all-gather | bytes 491520 | tf_op jit(solution)/shard_map/all_gather | solution.py:22
  46.5 3.7 %fusion.2 = f32[192,1024,2]{1,0,2:T(8,128)S(1)} fusion(bf16[128,2,8,1024]{3,2,1,0:T(8,128)(2,1)} %bitcast.77, bf16[1024,192]{0,1:T(8,128)(2,1)S(1)} %all_gather.10), kind=kOutput, calls=%fused_computation.2 | convolution fusion | flops 805306368 | bytes 6160384 | tf_op jit(solution)/shard_map/rick,kj->rcij/dot_general | solution.py:19
  50.3 1.7 fusion.7
  51.9 0.2 copy.24
  52.1 0.1 fusion.16
  52.2 23.6 %custom-call.17 = f32[1,2,128,128]{3,2,1,0:T(8,128)S(1)} custom-call(f32[1,2,128,128]{3,2,1,0:T(8,128)S(1)} %cholesky.132), custom_call_target="Cholesky" | custom-call | tf_op jit(solution)/shard_map/jit(cholesky)/cholesky | solution.py:26
  75.9 19.7 %custom-call.18 = f32[1,2,1,128,128]{3,4,2,1,0:T(8,128)S(1)} custom-call(f32[1,2,1,128,128]{4,3,2,1,0:T(8,128)S(1)} %get-tuple-element.26), custom_call_target="InvertDiagBlocksLowerTriangular" | custom-call | tf_op jit(solution)/shard_map/jit(cholesky)/cholesky | solution.py:26
  95.6 0.0 copy-start
  95.6 0.2 bitcast_dynamic-update-slice_fusion
  95.9 0.2 fusion.13
  96.1 11.7 %custom-call.19 = f32[1,2,64,64]{3,2,1,0:T(8,128)S(1)} custom-call(f32[1,2,64,64]{3,2,1,0:T(8,128)S(1)} %fusion.13), custom_call_target="Cholesky" | custom-call | tf_op jit(solution)/shard_map/jit(cholesky)/cholesky | solution.py:26
  107.9 0.1 compare_reduce_fusion
  108.0 0.1 compare_reduce_fusion.1
  108.1 0.1 bitcast_select_fusion
  108.3 0.1 fusion.18
  108.5 39.5 %custom-call.20 = f32[2,2,128,128]{2,3,1,0:T(8,128)S(1)} custom-call(f32[2,2,128,128]{3,2,1,0:T(8,128)S(1)} %pad_maximum_fusion), custom_call_target="InvertDiagBlocksLowerTriangular" | custom-call | tf_op jit(solution)/shard_map/jit(_solve_triangular)/vmap()/triangular_solve | solution.py:27
  148.0 0.0 copy-done
  148.0 0.1 compare_convert_fusion
  148.1 0.0 copy-start.1
  148.1 1.1 fusion.14
  149.2 0.7 convolution_subtract_fusion
  149.9 0.6 fusion.22
  150.5 0.0 copy-done.1
  150.5 2.0 fusion.9
  152.5 0.0 all-gather.2.cloned.1.call-done
  152.5 1.5 copy.30
  154.0 2.8 %fusion.12 = bf16[1024,256]{1,0:T(8,128)(2,1)} fusion(bf16[2,192,1024]{2,1,0:T(8,128)(2,1)} %fusion.9, bf16[2,1024,256]{2,1,0:T(8,128)(2,1)S(1)} %bitcast.75, f32[2,64,1024]{2,1,0:T(8,128)S(1)} %fusion.22, f32[2,128,1024]{2,1,0:T(8,128)S(1)} %fusion.14, f32[2,192]{1,0:T(2,128)S(1)} %compare_convert_fusion), kind=kOutput, calls=%fused_computation.12 | convolution fusion | flops 404193280 | bytes 3933696 | tf_op jit(solution)/shard_map/rcsi,rcsf->rif/dot_general | solution.py:41
  156.8 0.0 all-reduce.5.cloned.1.call-update
  156.8 73.5 %all-reduce.5.cloned.1.call-done = bf16[1024,256]{1,0:T(8,128)(2,1)} async-done(((bf16[1024,256]{1,0:T(8,128)(2,1)}), bf16[1024,256]{1,0:T(8,128)(2,1)}) %all-reduce.5.cloned.1.call-update) | async-done | bytes 524304 | tf_op jit(solution)/shard_map/psum | solution.py:42
  230.3 1.5 dynamic-slice_convert_fusion
  (14 shorter events, 0.2 us)
Async XLA Ops:
  6.5 146.0 %all-gather.2.cloned.1.call-start = ((), (), s32[]{:S(2)}) async-start(), calls=%async_computation | async-start | bytes 1310720 | tf_op jit(solution)/shard_map/all_gather | solution.py:8
  7.3 223.1 %all-reduce.5.cloned.1.call-start = ((), (), s32[]{:S(2)}) async-start(), calls=%async_computation.1 | async-start | bytes 1048576 | tf_op jit(solution)/shard_map/psum | solution.py:42
  95.6 52.4 %copy-start = (s32[1,2]{1,0:T(1,128)S(1)}, s32[1,2]{1,0:T(1,128)}, u32[]{:S(2)}) copy-start(s32[1,2]{1,0:T(1,128)} %param.7) | copy-start | bytes 28
  148.1 2.4 %copy-start.1 = (bf16[1024,2048]{1,0:T(8,128)(2,1)S(1)}, bf16[1024,2048]{1,0:T(8,128)(2,1)}, u32[]{:S(2)}) copy-start(bf16[1024,2048]{1,0:T(8,128)(2,1)} %param.4) | copy-start | bytes 12582916
Sparse Core Ops, SparseCore 0:
  8.9 19.4 all-gather.1
  156.9 73.3 all-reduce.4
where the time goes:
time: 239 us
  other arithmetic  96.8 us (41%)
  waiting for transfers between devices  74.2 us (31%)
  blocking collectives  39 us (16%)
  between operations  13.6 us (6%)
  matrix products  13 us (5%)
    psum x1, waiting for transfers between devices, on_device(): lax.psum(summed.reshape(tile_rows * width, frame_count).astype(jnp.bfloat...  73.5 us
    another operation x10, other arithmetic, on_device(): chol = jnp.linalg.cholesky(gram)  55.4 us
    another operation x7, other arithmetic, on_device(): jax.scipy.linalg.solve_triangular(chol, jnp.swapaxes(sketch, 2, 3), lower...  39.8 us
    all_gather x1, blocking collectives, on_device(): row_block = lax.all_gather(test_matrix, 'tcol', axis=0, tiled=True)  32.5 us
    all_gather x1, blocking collectives, on_device(): lax.all_gather(row_block, 'trow', axis=0, tiled=True)  6.49 us
  transfers between devices with their start and end apart: 2, of which 1 were waited for; matrix products, arithmetic and copies ran while one was open for 44% of the time, Pallas kernels for 0%

commit v1 on v0

v1 whole, which is shorter than its diff:
```python
import functools

import jax
import jax.numpy as jnp
from jax import lax
from jax.experimental import pallas as pl
from jax.experimental.pallas import tpu as pltpu
from jax.sharding import PartitionSpec as P

MESH = pl.DeviceIdType.MESH
F32 = jnp.float32
BF16 = jnp.bfloat16
HIGHEST = lax.Precision.HIGHEST
BLOCK = 64


def dot(a, b, ca, cb, precision=None):
    return lax.dot_general(
        a, b, (((ca,), (cb,)), ((), ())), precision=precision, preferred_element_type=F32
    )


def split_halves(x, low):
    zero = jnp.zeros_like(x)
    return jnp.concatenate([jnp.where(low, x, zero), jnp.where(low, zero, x)], axis=0)


def invert_block(x):
    lane = lax.broadcasted_iota(jnp.int32, x.shape, 1)
    for k in range(BLOCK):
        where = jnp.where(lane < BLOCK, k, BLOCK + k)
        column = jnp.take_along_axis(x, where, axis=1)
        row = x[k : k + 1, :]
        pivot = column[k : k + 1, :]
        x = x - column * (row * (1.0 / (1.0 + pivot)))
    return x


def kernel(
    nr, nc, resp, tm, sl, ranks, out,
    a_v, om, own, fr, s_b, w_v, b_v, part, land,
    a_sem, o_sem, f_sem, s1, r1, s2, r2, s3, r3, s4, r4,
):
    r, c = lax.axis_index("trow"), lax.axis_index("tcol")
    width = a_v.shape[0]
    sketch = tm.shape[1]
    blocks = sketch // BLOCK
    tile_cols = a_v.shape[1] // width
    local = sl.shape[1]
    load_a = pltpu.make_async_copy(resp, a_v, a_sem)
    load_a.start()
    own_om = pltpu.make_async_copy(tm, om.at[r, c], o_sem)
    own_om.start()
    for t in range(tile_cols):
        own[:, t * local : (t + 1) * local] = sl[t * width : (t + 1) * width, :]
    barrier = pltpu.get_barrier_semaphore()
    for d in range(1, nc):
        pl.semaphore_signal(barrier, inc=1, device_id=(r, lax.rem(c + d, nc)), device_id_type=MESH)
    for e in range(1, nr):
        pl.semaphore_signal(barrier, inc=1, device_id=(lax.rem(r + e, nr), c), device_id_type=MESH)
    pl.semaphore_wait(barrier, nc - 1 + nr - 1)
    first = []
    for d in range(1, nc):
        cp = pltpu.make_async_remote_copy(
            tm, om.at[r, c], s1.at[d - 1], r1.at[d - 1],
            device_id=(r, lax.rem(c + d, nc)), device_id_type=MESH,
        )
        cp.start()
        first.append(cp)
    own_om.wait()
    for cp in first:
        cp.wait_recv()
    second, third = [], []
    for e in range(1, nr):
        cp = pltpu.make_async_remote_copy(
            om.at[r], om.at[r], s2.at[e - 1], r2.at[e - 1],
            device_id=(lax.rem(r + e, nr), c), device_id_type=MESH,
        )
        cp.start()
        second.append(cp)
    own_fr = pltpu.make_async_copy(own, fr.at[r], f_sem)
    own_fr.start()
    for e in range(1, nr):
        cp = pltpu.make_async_remote_copy(
            own, fr.at[r], s3.at[e - 1], r3.at[e - 1],
            device_id=(lax.rem(r + e, nr), c), device_id_type=MESH,
        )
        cp.start()
        third.append(cp)
    load_a.wait()
    for cp in second:
        cp.wait_recv()
    omega = om[...].astype(F32).reshape(width, sketch).astype(BF16)

    slot = lax.broadcasted_iota(jnp.int32, (1, sketch), 1)
    grams = []
    for t in range(tile_cols):
        s = dot(a_v[:, t * width : (t + 1) * width], omega, 1, 0)
        norm = jnp.sum(s * s, axis=0, keepdims=True)
        scale = jnp.where(slot < ranks[0, t], lax.rsqrt(norm), 0.0)
        hat = (s * scale).astype(BF16)
        s_b[t] = hat
        grams.append(dot(hat, hat, 0, 0))

    half = lax.broadcasted_iota(jnp.int32, (sketch, 2 * BLOCK), 1)
    rows = lax.broadcasted_iota(jnp.int32, (sketch, 2 * BLOCK), 0)
    low = half < BLOCK
    for j in range(blocks):
        x = jnp.concatenate([g[:, j * BLOCK : (j + 1) * BLOCK] for g in grams], axis=1)
        index = jnp.where(low, half, half - BLOCK) + j * BLOCK
        limit = jnp.where(low, ranks[0, 0], ranks[0, 1])
        b_v[j] = jnp.where((rows == index) & (index < limit), x - 1.0, x)

    low_b = lax.broadcasted_iota(jnp.int32, (BLOCK, 2 * BLOCK), 1) < BLOCK
    for k in range(blocks):
        span = slice(k * BLOCK, (k + 1) * BLOCK)
        square = invert_block(b_v[k, span, :])
        whole_k = b_v[k]
        mid = whole_k - dot(whole_k, split_halves(square, low_b), 1, 0, HIGHEST)
        rights = [split_halves(b_v[j, span, :], low_b) for j in range(blocks)]
        for j in range(blocks):
            b_v[j] = b_v[j] - dot(mid, rights[j], 1, 0, HIGHEST)

    own_fr.wait()
    for cp in third:
        cp.wait_recv()
    frames = nr * local
    for t in range(tile_cols):
        s_t = jnp.concatenate(
            [fr[q, :, t * local : (t + 1) * local] for q in range(nr)], axis=1
        )
        y = dot(a_v[:, t * width : (t + 1) * width], s_t, 1, 0).astype(BF16)
        w_v[t] = dot(s_b[t], y, 0, 0)

    full = jnp.concatenate([b_v[j] for j in range(blocks)], axis=1)
    stack = []
    for j in range(blocks):
        span = slice(j * BLOCK, (j + 1) * BLOCK)
        w0, w1 = w_v[0, span, :], w_v[1, span, :]
        zero = jnp.zeros_like(w0)
        stack.append(jnp.concatenate([w0, zero], axis=1))
        stack.append(jnp.concatenate([zero, w1], axis=1))
    corr = dot(full, jnp.concatenate(stack, axis=0), 1, 0, HIGHEST)
    ds = [
        (w_v[t] - corr[:, t * frames : (t + 1) * frames]).astype(BF16) for t in range(tile_cols)
    ]

    share = width // nc
    sends = []

    def chunk(at):
        rows_at = pl.ds(pl.multiple_of(at * share, share), share)
        return sum(dot(s_b[t, rows_at, :], ds[t], 1, 0) for t in range(tile_cols))

    for d in range(1, nc):
        to = lax.rem(c + d, nc)
        part[d - 1] = chunk(to).astype(BF16)
        cp = pltpu.make_async_remote_copy(
            part.at[d - 1], land.at[d - 1], s4.at[d - 1], r4.at[d - 1],
            device_id=(r, to), device_id_type=MESH,
        )
        sends.append(cp)
        if d > 1:
            sends[d - 2].start()
    total = chunk(c)
    sends[-1].start()
    for cp, n in zip(sends, range(nc)):
        cp.wait_recv()
        total = total + land[n].astype(F32)
    out[...] = total
    for cp in first + second + third + sends:
        cp.wait_send()


def on_device(nr, nc, response, test_matrix, slopes, ranks):
    rows, cols = response.shape
    tile_rows, tile_cols = ranks.shape
    width = rows // tile_rows
    m, sketch = test_matrix.shape
    local = slopes.shape[1]
    frames = local * nr
    share = width // nc
    dma = pltpu.SemaphoreType.DMA
    return pl.pallas_call(
        functools.partial(kernel, nr, nc),
        out_shape=jax.ShapeDtypeStruct((share, frames), F32),
        in_specs=[
            pl.BlockSpec(memory_space=pl.ANY),
            pl.BlockSpec(memory_space=pltpu.VMEM),
            pl.BlockSpec(memory_space=pltpu.VMEM),
            pl.BlockSpec(memory_space=pltpu.SMEM),
        ],
        out_specs=pl.BlockSpec(memory_space=pltpu.VMEM),
        scratch_shapes=[
            pltpu.VMEM((rows, cols), BF16),
            pltpu.VMEM((nr, nc, m, sketch), BF16),
            pltpu.VMEM((width, tile_cols * local), BF16),
            pltpu.VMEM((nr, width, tile_cols * local), BF16),
            pltpu.VMEM((tile_cols, width, sketch), BF16),
            pltpu.VMEM((tile_cols, sketch, frames), F32),
            pltpu.VMEM((sketch // BLOCK, sketch, 2 * BLOCK), F32),
            pltpu.VMEM((nc - 1, share, frames), BF16),
            pltpu.VMEM((nc - 1, share, frames), BF16),
            dma, dma, dma,
            dma((nc - 1,)), dma((nc - 1,)),
            dma((nr - 1,)), dma((nr - 1,)),
            dma((nr - 1,)), dma((nr - 1,)),
            dma((nc - 1,)), dma((nc - 1,)),
        ],
        compiler_params=pltpu.CompilerParams(
            collective_id=0, has_side_effects=True, vmem_limit_bytes=60 * 1024 * 1024
        ),
    )(response, test_matrix, slopes, ranks)


def solution(mesh):
    nr, nc = mesh.shape["trow"], mesh.shape["tcol"]
    return jax.shard_map(
        functools.partial(on_device, nr, nc),
        mesh=mesh,
        in_specs=(
            P("trow", "tcol"),
            P(("trow", "tcol"), None),
            P("tcol", "trow"),
            P("trow", "tcol"),
        ),
        out_specs=P(("trow", "tcol"), None),
        check_vma=False,
    )
```

time: 239 us -> 59.5 us (0.25)
  the two profiles are of different devices: /device:TPU:0 before, /device:TPU:9 now
where the time goes in v1:
time: 59.5 us; the launch traced here: 59.3 us
  Pallas kernels  55.7 us (94%)
  local copies, waits for them, and re-layouts  3.52 us (6%)
    pallas_call x1, Pallas kernels, on_device(): pl.pallas_call(functools.partial(kernel, nr, nc), out_shape=jax.ShapeDtyp...  55.7 us
    unnamed x2, local copies, waits for them, and re-layouts  3.52 us

profile of v1, /device:TPU:9, one launch (start us, length us, event | category | flops | bytes accessed | tf_op | source)
XLA Modules:
  0.0 59.3 jit_solution(5008260301500072682)
XLA Ops:
  0.0 1.9 %copy.5.sl = bf16[2048,64]{1,0:T(8,128)(2,1)} copy(bf16[2048,64]{0,1:T(8,128)(2,1)} %param.6) | data formatting | bytes 524288 | tf_op args[2]
  1.9 55.7 %shard_map.46 = f32[128,256]{1,0:T(8,128)} custom-call(bf16[1024,2048]{1,0:T(8,128)(2,1)} %resp.1, bf16[32,192]{1,0:T(8,128)(2,1)} %tm.1, bf16[2048,64]{1,0:T(8,128)(2,1)} %copy.5.sl, s32[1,2]{1,0:T(1,128)} %ranks.1), custom_call_target="tpu_custom_call" | custom-call | tf_op jit(solution)/shard_map/pallas_call | solution.py:184
  57.7 1.6 %copy.7 = f32[128,256]{1,0:T(8,128)} copy(f32[128,256]{1,0:T(8,128)} %shard_map.46) | data formatting | bytes 262144

commit v2 on v1

--- a/solution.py
+++ b/solution.py
@@ -12,6 +12,7 @@
 BF16 = jnp.bfloat16
 HIGHEST = lax.Precision.HIGHEST
 BLOCK = 64
+PANEL = 8
 
 
 def dot(a, b, ca, cb, precision=None):
@@ -26,33 +27,56 @@
 
 
 def invert_block(x):
-    lane = lax.broadcasted_iota(jnp.int32, x.shape, 1)
-    for k in range(BLOCK):
-        where = jnp.where(lane < BLOCK, k, BLOCK + k)
-        column = jnp.take_along_axis(x, where, axis=1)
-        row = x[k : k + 1, :]
-        pivot = column[k : k + 1, :]
-        x = x - column * (row * (1.0 / (1.0 + pivot)))
+    base = jnp.where(lax.broadcasted_iota(jnp.int32, (PANEL, x.shape[1]), 1) < BLOCK, 0, BLOCK)
+    for at in range(0, BLOCK, PANEL):
+        picks = [base + (at + i) for i in range(PANEL)]
+        rows = x[at : at + PANEL, :]
+        cols = [jnp.take_along_axis(rows, pick, axis=1) for pick in picks]
+        for i in range(0, PANEL, 2):
+            c0, c1 = cols[i], cols[i + 1]
+            p00 = 1.0 + c0[i : i + 1, :]
+            p01 = c1[i : i + 1, :]
+            p11 = 1.0 + c1[i + 1 : i + 2, :]
+            inv = 1.0 / (p00 * p11 - p01 * p01)
+            m00, m01, m11 = p11 * inv, -p01 * inv, p00 * inv
+
+            def clear(v):
+                v0, v1 = v[i : i + 1, :], v[i + 1 : i + 2, :]
+                return v - (c0 * (m00 * v0 + m01 * v1) + c1 * (m01 * v0 + m11 * v1))
+
+            rows = clear(rows)
+            for j in range(i + 2, PANEL):
+                cols[j] = clear(cols[j])
+        pieces = []
+        for top in range(0, BLOCK, PANEL):
+            piece = x[top : top + PANEL, :]
+            delta = None
+            for i in range(PANEL):
+                term = jnp.take_along_axis(piece, picks[i], axis=1) * rows[i : i + 1, :]
+                delta = term if delta is None else delta + term
+            pieces.append(piece - delta)
+        x = jnp.concatenate(pieces, axis=0)
     return x
 
 
 def kernel(
     nr, nc, resp, tm, sl, ranks, out,
-    a_v, om, own, fr, s_b, w_v, b_v, part, land,
-    a_sem, o_sem, f_sem, s1, r1, s2, r2, s3, r3, s4, r4,
+    a_v, om, fr, s_v, s_b, s_t, w_v, b_v, keep, part1, land1, part2, land2,
+    a_sem, o_sem, f_sem, s1, r1, s2, r2, s3, r3, s4, r4, s5, r5,
 ):
     r, c = lax.axis_index("trow"), lax.axis_index("tcol")
     width = a_v.shape[0]
     sketch = tm.shape[1]
     blocks = sketch // BLOCK
     tile_cols = a_v.shape[1] // width
-    local = sl.shape[1]
+    local = sl.shape[0]
+    deep = width // nr
     load_a = pltpu.make_async_copy(resp, a_v, a_sem)
     load_a.start()
     own_om = pltpu.make_async_copy(tm, om.at[r, c], o_sem)
     own_om.start()
-    for t in range(tile_cols):
-        own[:, t * local : (t + 1) * local] = sl[t * width : (t + 1) * width, :]
+    own_fr = pltpu.make_async_copy(sl, fr.at[r], f_sem)
+    own_fr.start()
     barrier = pltpu.get_barrier_semaphore()
     for d in range(1, nc):
         pl.semaphore_signal(barrier, inc=1, device_id=(r, lax.rem(c + d, nc)), device_id_type=MESH)
@@ -70,37 +94,61 @@
     own_om.wait()
     for cp in first:
         cp.wait_recv()
-    second, third = [], []
-    for e in range(1, nr):
+
+    mate = r + 1 - 2 * lax.rem(r, 2)
+    far = nr // 2
+
+    def shift(e):
+        return lax.rem(r + 2 * e, nr)
+
+    def unshift(e):
+        return lax.rem(r - 2 * e + nr, nr)
+
+    def push(src, dst, send, recv, n, to):
         cp = pltpu.make_async_remote_copy(
-            om.at[r], om.at[r], s2.at[e - 1], r2.at[e - 1],
-            device_id=(lax.rem(r + e, nr), c), device_id_type=MESH,
+            src, dst, send.at[n], recv.at[n], device_id=(to, c), device_id_type=MESH
         )
         cp.start()
-        second.append(cp)
-    own_fr = pltpu.make_async_copy(own, fr.at[r], f_sem)
-    own_fr.start()
-    for e in range(1, nr):
-        cp = pltpu.make_async_remote_copy(
-            own, fr.at[r], s3.at[e - 1], r3.at[e - 1],
-            device_id=(lax.rem(r + e, nr), c), device_id_type=MESH,
-        )
-        cp.start()
-        third.append(cp)
+        return cp
+
+    second = [push(om.at[r], om.at[r], s2, r2, e, shift(e)) for e in range(1, far)]
+    second.insert(0, push(om.at[r], om.at[r], s2, r2, 0, mate))
+    third = [push(sl, fr.at[r], s3, r3, e, shift(e)) for e in range(1, far)]
+    third.insert(0, push(sl, fr.at[r], s3, r3, 0, mate))
     load_a.wait()
-    for cp in second:
-        cp.wait_recv()
-    omega = om[...].astype(F32).reshape(width, sketch).astype(BF16)
+
+    def add_block(q, fresh):
+        omega = om[q].astype(F32).reshape(deep, sketch).astype(BF16)
+        for t in range(tile_cols):
+            at = pl.ds(pl.multiple_of(t * width + q * deep, 128), deep)
+            term = dot(a_v[:, at], omega, 1, 0)
+            s_v[t] = term if fresh else s_v[t] + term
+
+    add_block(r, True)
+    for e in range(1, far):
+        second[e].wait_recv()
+        q = unshift(e)
+        second.append(push(om.at[q], om.at[q], s2, r2, far - 1 + e, mate))
+    second[0].wait_recv()
+    add_block(mate, False)
+    for e in range(1, far):
+        add_block(unshift(e), False)
+    for e in range(1, far):
+        second[far - 1 + e].wait_recv()
+        q = unshift(e)
+        add_block(q + 1 - 2 * lax.rem(q, 2), False)
 
     slot = lax.broadcasted_iota(jnp.int32, (1, sketch), 1)
     grams = []
     for t in range(tile_cols):
-        s = dot(a_v[:, t * width : (t + 1) * width], omega, 1, 0)
+        s = s_v[t]
         norm = jnp.sum(s * s, axis=0, keepdims=True)
         scale = jnp.where(slot < ranks[0, t], lax.rsqrt(norm), 0.0)
         hat = (s * scale).astype(BF16)
         s_b[t] = hat
-        grams.append(dot(hat, hat, 0, 0))
+        turned = hat.T
+        s_t[t] = turned
+        grams.append(dot(turned, hat, 1, 0))
 
     half = lax.broadcasted_iota(jnp.int32, (sketch, 2 * BLOCK), 1)
     rows = lax.broadcasted_iota(jnp.int32, (sketch, 2 * BLOCK), 0)
@@ -120,17 +168,21 @@
         rights = [split_halves(b_v[j, span, :], low_b) for j in range(blocks)]
         for j in range(blocks):
             b_v[j] = b_v[j] - dot(mid, rights[j], 1, 0, HIGHEST)
+        if k == 0:
+            for e in range(1, far):
+                third[e].wait_recv()
+                q = unshift(e)
+                third.append(push(fr.at[q], fr.at[q], s3, r3, far - 1 + e, mate))
 
     own_fr.wait()
-    for cp in third:
-        cp.wait_recv()
+    third[0].wait_recv()
+    for e in range(1, far):
+        third[far - 1 + e].wait_recv()
     frames = nr * local
     for t in range(tile_cols):
-        s_t = jnp.concatenate(
-            [fr[q, :, t * local : (t + 1) * local] for q in range(nr)], axis=1
-        )
-        y = dot(a_v[:, t * width : (t + 1) * width], s_t, 1, 0).astype(BF16)
-        w_v[t] = dot(s_b[t], y, 0, 0)
+        s = fr[:, :, t * width : (t + 1) * width].reshape(frames, width)
+        y = dot(a_v[:, t * width : (t + 1) * width], s, 1, 1).astype(BF16)
+        w_v[t] = dot(s_t[t], y, 1, 0)
 
     full = jnp.concatenate([b_v[j] for j in range(blocks)], axis=1)
     stack = []
@@ -146,29 +198,45 @@
     ]
 
     share = width // nc
-    sends = []
+    pairs = nc // 2
+    side = lax.rem(c, 2)
+    near = c + 1 - 2 * side
+    order = list(range(1, pairs)) + [0]
+
+    def group(e):
+        return 2 * lax.rem(c // 2 + e, pairs)
 
     def chunk(at):
         rows_at = pl.ds(pl.multiple_of(at * share, share), share)
         return sum(dot(s_b[t, rows_at, :], ds[t], 1, 0) for t in range(tile_cols))
 
-    for d in range(1, nc):
-        to = lax.rem(c + d, nc)
-        part[d - 1] = chunk(to).astype(BF16)
+    across = []
+    for n, e in enumerate(order):
+        part1[n] = chunk(group(e) + 1 - side).astype(BF16)
+        keep[n] = chunk(group(e) + side)
         cp = pltpu.make_async_remote_copy(
-            part.at[d - 1], land.at[d - 1], s4.at[d - 1], r4.at[d - 1],
-            device_id=(r, to), device_id_type=MESH,
+            part1.at[n], land1.at[n], s4.at[n], r4.at[n],
+            device_id=(r, near), device_id_type=MESH,
         )
-        sends.append(cp)
-        if d > 1:
-            sends[d - 2].start()
-    total = chunk(c)
-    sends[-1].start()
-    for cp, n in zip(sends, range(nc)):
-        cp.wait_recv()
-        total = total + land[n].astype(F32)
+        cp.start()
+        across.append(cp)
+    along = []
+    for n in range(pairs - 1):
+        across[n].wait_recv()
+        part2[n] = (keep[n] + land1[n].astype(F32)).astype(BF16)
+        cp = pltpu.make_async_remote_copy(
+            part2.at[n], land2.at[n], s5.at[n], r5.at[n],
+            device_id=(r, group(order[n]) + side), device_id_type=MESH,
+        )
+        cp.start()
+        along.append(cp)
+    across[-1].wait_recv()
+    total = keep[pairs - 1] + land1[pairs - 1].astype(F32)
+    for n in range(pairs - 1):
+        along[n].wait_recv()
+        total = total + land2[n].astype(F32)
     out[...] = total
-    for cp in first + second + third + sends:
+    for cp in first + second + third + across + along:
         cp.wait_send()
 
 
@@ -177,9 +245,11 @@
     tile_rows, tile_cols = ranks.shape
     width = rows // tile_rows
     m, sketch = test_matrix.shape
-    local = slopes.shape[1]
+    slopes = slopes.T
+    local = slopes.shape[0]
     frames = local * nr
     share = width // nc
+    pairs = nc // 2
     dma = pltpu.SemaphoreType.DMA
     return pl.pallas_call(
         functools.partial(kernel, nr, nc),
@@ -194,18 +264,23 @@
         scratch_shapes=[
             pltpu.VMEM((rows, cols), BF16),
             pltpu.VMEM((nr, nc, m, sketch), BF16),
-            pltpu.VMEM((width, tile_cols * local), BF16),
-            pltpu.VMEM((nr, width, tile_cols * local), BF16),
+            pltpu.VMEM((nr, local, cols), BF16),
+            pltpu.VMEM((tile_cols, width, sketch), F32),
             pltpu.VMEM((tile_cols, width, sketch), BF16),
+            pltpu.VMEM((tile_cols, sketch, width), BF16),
             pltpu.VMEM((tile_cols, sketch, frames), F32),
             pltpu.VMEM((sketch // BLOCK, sketch, 2 * BLOCK), F32),
-            pltpu.VMEM((nc - 1, share, frames), BF16),
-            pltpu.VMEM((nc - 1, share, frames), BF16),
+            pltpu.VMEM((pairs, share, frames), F32),
+            pltpu.VMEM((pairs, share, frames), BF16),
+            pltpu.VMEM((pairs, share, frames), BF16),
+            pltpu.VMEM((pairs - 1, share, frames), BF16),
+            pltpu.VMEM((pairs - 1, share, frames), BF16),
             dma, dma, dma,
             dma((nc - 1,)), dma((nc - 1,)),
             dma((nr - 1,)), dma((nr - 1,)),
             dma((nr - 1,)), dma((nr - 1,)),
-            dma((nc - 1,)), dma((nc - 1,)),
+            dma((pairs,)), dma((pairs,)),
+            dma((pairs - 1,)), dma((pairs - 1,)),
         ],
         compiler_params=pltpu.CompilerParams(
             collective_id=0, has_side_effects=True, vmem_limit_bytes=60 * 1024 * 1024

time: 59.5 us -> 46.8 us (0.79)
  the two profiles are of different devices: /device:TPU:9 before, /device:TPU:0 now
where the time goes in v2:
time: 46.8 us; the launch traced here: 46.6 us
  Pallas kernels  45 us (96%)
  local copies, waits for them, and re-layouts  1.57 us (3%)
    pallas_call x1, Pallas kernels, on_device(): pl.pallas_call(functools.partial(kernel, nr, nc), out_shape=jax.ShapeDtyp...  45 us
    unnamed x1, local copies, waits for them, and re-layouts  1.57 us

profile of v2, /device:TPU:0, one launch (start us, length us, event | category | flops | bytes accessed | tf_op | source)
XLA Modules:
  0.0 46.6 jit_solution(17736808453296775765)
XLA Ops:
  0.0 45.0 %shard_map.46 = f32[128,256]{1,0:T(8,128)} custom-call(bf16[1024,2048]{1,0:T(8,128)(2,1)} %resp.1, bf16[32,192]{1,0:T(8,128)(2,1)} %tm.1, bf16[64,2048]{1,0:T(8,128)(2,1)} %bitcast.1, s32[1,2]{1,0:T(1,128)} %ranks.1), custom_call_target="tpu_custom_call" | custom-call | tf_op jit(solution)/shard_map/pallas_call | solution.py:254
  45.0 1.6 %copy.6 = f32[128,256]{1,0:T(8,128)} copy(f32[128,256]{1,0:T(8,128)} %shard_map.46) | data formatting | bytes 262144

commit v3 on v2

--- a/solution.py
+++ b/solution.py
@@ -10,7 +10,6 @@
 MESH = pl.DeviceIdType.MESH
 F32 = jnp.float32
 BF16 = jnp.bfloat16
-HIGHEST = lax.Precision.HIGHEST
 BLOCK = 64
 PANEL = 8
 
@@ -19,6 +18,26 @@
     return lax.dot_general(
         a, b, (((ca,), (cb,)), ((), ())), precision=precision, preferred_element_type=F32
     )
+
+
+def split(a):
+    high = a.astype(BF16)
+    return high, (a - high.astype(F32)).astype(BF16)
+
+
+def dot3(a, b):
+    a0, a1 = split(a)
+    b0, b1 = split(b)
+    return dot(a0, b0, 1, 0) + (dot(a0, b1, 1, 0) + dot(a1, b0, 1, 0))
+
+
+def flip(a, mask):
+    bit, result = 1, a
+    while bit <= mask:
+        if mask & bit:
+            result = result + bit - 2 * bit * lax.rem(a // bit, 2)
+        bit *= 2
+    return result
 
 
 def split_halves(x, low):
@@ -159,30 +178,34 @@
         limit = jnp.where(low, ranks[0, 0], ranks[0, 1])
         b_v[j] = jnp.where((rows == index) & (index < limit), x - 1.0, x)
 
+    frames = nr * local
+
+    def apply_frames():
+        own_fr.wait()
+        third[0].wait_recv()
+        for e in range(1, far):
+            third[far - 1 + e].wait_recv()
+        for t in range(tile_cols):
+            s = fr[:, :, t * width : (t + 1) * width].reshape(frames, width)
+            y = dot(a_v[:, t * width : (t + 1) * width], s, 1, 1).astype(BF16)
+            w_v[t] = dot(s_t[t], y, 1, 0)
+
     low_b = lax.broadcasted_iota(jnp.int32, (BLOCK, 2 * BLOCK), 1) < BLOCK
     for k in range(blocks):
         span = slice(k * BLOCK, (k + 1) * BLOCK)
+        if k == blocks - 1:
+            apply_frames()
         square = invert_block(b_v[k, span, :])
         whole_k = b_v[k]
-        mid = whole_k - dot(whole_k, split_halves(square, low_b), 1, 0, HIGHEST)
+        mid = whole_k - dot3(whole_k, split_halves(square, low_b))
         rights = [split_halves(b_v[j, span, :], low_b) for j in range(blocks)]
         for j in range(blocks):
-            b_v[j] = b_v[j] - dot(mid, rights[j], 1, 0, HIGHEST)
+            b_v[j] = b_v[j] - dot3(mid, rights[j])
         if k == 0:
             for e in range(1, far):
                 third[e].wait_recv()
                 q = unshift(e)
                 third.append(push(fr.at[q], fr.at[q], s3, r3, far - 1 + e, mate))
-
-    own_fr.wait()
-    third[0].wait_recv()
-    for e in range(1, far):
-        third[far - 1 + e].wait_recv()
-    frames = nr * local
-    for t in range(tile_cols):
-        s = fr[:, :, t * width : (t + 1) * width].reshape(frames, width)
-        y = dot(a_v[:, t * width : (t + 1) * width], s, 1, 1).astype(BF16)
-        w_v[t] = dot(s_t[t], y, 1, 0)
 
     full = jnp.concatenate([b_v[j] for j in range(blocks)], axis=1)
     stack = []
@@ -192,7 +215,7 @@
         zero = jnp.zeros_like(w0)
         stack.append(jnp.concatenate([w0, zero], axis=1))
         stack.append(jnp.concatenate([zero, w1], axis=1))
-    corr = dot(full, jnp.concatenate(stack, axis=0), 1, 0, HIGHEST)
+    corr = dot3(full, jnp.concatenate(stack, axis=0))
     ds = [
         (w_v[t] - corr[:, t * frames : (t + 1) * frames]).astype(BF16) for t in range(tile_cols)
     ]
@@ -201,41 +224,47 @@
     pairs = nc // 2
     side = lax.rem(c, 2)
     near = c + 1 - 2 * side
-    order = list(range(1, pairs)) + [0]
-
-    def group(e):
-        return 2 * lax.rem(c // 2 + e, pairs)
+    halves = frames // 2
+    cuts = [slice(0, halves), slice(halves, frames)]
+
+    def group(n):
+        return 2 * flip(c // 2, pairs - 1 - n)
 
     def chunk(at):
         rows_at = pl.ds(pl.multiple_of(at * share, share), share)
         return sum(dot(s_b[t, rows_at, :], ds[t], 1, 0) for t in range(tile_cols))
 
     across = []
-    for n, e in enumerate(order):
-        part1[n] = chunk(group(e) + 1 - side).astype(BF16)
-        keep[n] = chunk(group(e) + side)
-        cp = pltpu.make_async_remote_copy(
-            part1.at[n], land1.at[n], s4.at[n], r4.at[n],
-            device_id=(r, near), device_id_type=MESH,
-        )
-        cp.start()
-        across.append(cp)
+    for n in range(pairs):
+        piece = chunk(group(n) + 1 - side).astype(BF16)
+        for h in range(2):
+            part1[n, h] = piece[:, cuts[h]]
+        keep[n] = chunk(group(n) + side)
+        for h in range(2):
+            cp = pltpu.make_async_remote_copy(
+                part1.at[n, h], land1.at[n, h], s4.at[n, h], r4.at[n, h],
+                device_id=(r, near), device_id_type=MESH,
+            )
+            cp.start()
+            across.append(cp)
     along = []
     for n in range(pairs - 1):
-        across[n].wait_recv()
-        part2[n] = (keep[n] + land1[n].astype(F32)).astype(BF16)
-        cp = pltpu.make_async_remote_copy(
-            part2.at[n], land2.at[n], s5.at[n], r5.at[n],
-            device_id=(r, group(order[n]) + side), device_id_type=MESH,
-        )
-        cp.start()
-        along.append(cp)
-    across[-1].wait_recv()
-    total = keep[pairs - 1] + land1[pairs - 1].astype(F32)
-    for n in range(pairs - 1):
-        along[n].wait_recv()
-        total = total + land2[n].astype(F32)
-    out[...] = total
+        for h in range(2):
+            across[2 * n + h].wait_recv()
+            part2[n, h] = (keep[n, :, cuts[h]] + land1[n, h].astype(F32)).astype(BF16)
+            cp = pltpu.make_async_remote_copy(
+                part2.at[n, h], land2.at[n, h], s5.at[n, h], r5.at[n, h],
+                device_id=(r, group(n) + side), device_id_type=MESH,
+            )
+            cp.start()
+            along.append(cp)
+    for h in range(2):
+        across[2 * (pairs - 1) + h].wait_recv()
+        total = keep[pairs - 1, :, cuts[h]] + land1[pairs - 1, h].astype(F32)
+        for n in range(pairs - 1):
+            along[2 * n + h].wait_recv()
+            total = total + land2[n, h].astype(F32)
+        out[:, cuts[h]] = total
     for cp in first + second + third + across + along:
         cp.wait_send()
 
@@ -271,16 +300,16 @@
             pltpu.VMEM((tile_cols, sketch, frames), F32),
             pltpu.VMEM((sketch // BLOCK, sketch, 2 * BLOCK), F32),
             pltpu.VMEM((pairs, share, frames), F32),
-            pltpu.VMEM((pairs, share, frames), BF16),
-            pltpu.VMEM((pairs, share, frames), BF16),
-            pltpu.VMEM((pairs - 1, share, frames), BF16),
-            pltpu.VMEM((pairs - 1, share, frames), BF16),
+            pltpu.VMEM((pairs, 2, share, frames // 2), BF16),
+            pltpu.VMEM((pairs, 2, share, frames // 2), BF16),
+            pltpu.VMEM((pairs - 1, 2, share, frames // 2), BF16),
+            pltpu.VMEM((pairs - 1, 2, share, frames // 2), BF16),
             dma, dma, dma,
             dma((nc - 1,)), dma((nc - 1,)),
             dma((nr - 1,)), dma((nr - 1,)),
             dma((nr - 1,)), dma((nr - 1,)),
-            dma((pairs,)), dma((pairs,)),
-            dma((pairs - 1,)), dma((pairs - 1,)),
+            dma((pairs, 2)), dma((pairs, 2)),
+            dma((pairs - 1, 2)), dma((pairs - 1, 2)),
         ],
         compiler_params=pltpu.CompilerParams(
             collective_id=0, has_side_effects=True, vmem_limit_bytes=60 * 1024 * 1024

time: 46.8 us -> 42.8 us (0.915)
  Pallas kernels: 45 us -> 41 us
    pallas_call x1, Pallas kernels: 45 us -> 41 us  [on_device(): pl.pallas_call(functools.partial(kernel, nr, nc), out_shape=jax.ShapeDtyp...]
where the time goes in v3:
time: 42.8 us; the launch traced here: 42.5 us
  Pallas kernels  41 us (96%)
  local copies, waits for them, and re-layouts  1.57 us (4%)
    pallas_call x1, Pallas kernels, on_device(): pl.pallas_call(functools.partial(kernel, nr, nc), out_shape=jax.ShapeDtyp...  41 us
    unnamed x1, local copies, waits for them, and re-layouts  1.57 us

profile of v3, /device:TPU:0, one launch (start us, length us, event | category | flops | bytes accessed | tf_op | source)
XLA Modules:
  0.0 42.5 jit_solution(8227332216193380002)
XLA Ops:
  0.0 41.0 %shard_map.46 = f32[128,256]{1,0:T(8,128)} custom-call(bf16[1024,2048]{1,0:T(8,128)(2,1)} %resp.1, bf16[32,192]{1,0:T(8,128)(2,1)} %tm.1, bf16[64,2048]{1,0:T(8,128)(2,1)} %bitcast.1, s32[1,2]{1,0:T(1,128)} %ranks.1), custom_call_target="tpu_custom_call" | custom-call | tf_op jit(solution)/shard_map/pallas_call | solution.py:283
  41.0 1.6 %copy.6 = f32[128,256]{1,0:T(8,128)} copy(f32[128,256]{1,0:T(8,128)} %shard_map.46) | data formatting | bytes 262144

commit v4 on v3

--- a/solution.py
+++ b/solution.py
@@ -11,7 +11,7 @@
 F32 = jnp.float32
 BF16 = jnp.bfloat16
 BLOCK = 64
-PANEL = 8
+PANEL = 16
 
 
 def dot(a, b, ca, cb, precision=None):
@@ -207,18 +207,12 @@
                 q = unshift(e)
                 third.append(push(fr.at[q], fr.at[q], s3, r3, far - 1 + e, mate))
 
-    full = jnp.concatenate([b_v[j] for j in range(blocks)], axis=1)
-    stack = []
-    for j in range(blocks):
-        span = slice(j * BLOCK, (j + 1) * BLOCK)
-        w0, w1 = w_v[0, span, :], w_v[1, span, :]
-        zero = jnp.zeros_like(w0)
-        stack.append(jnp.concatenate([w0, zero], axis=1))
-        stack.append(jnp.concatenate([zero, w1], axis=1))
-    corr = dot3(full, jnp.concatenate(stack, axis=0))
-    ds = [
-        (w_v[t] - corr[:, t * frames : (t + 1) * frames]).astype(BF16) for t in range(tile_cols)
-    ]
+    ds = []
+    for t in range(tile_cols):
+        mine = slice(t * BLOCK, (t + 1) * BLOCK)
+        full = jnp.concatenate([b_v[j, :, mine] for j in range(blocks)], axis=1)
+        w = w_v[t]
+        ds.append((w - dot3(full, w)).astype(BF16))
 
     share = width // nc
     pairs = nc // 2

time: 42.8 us -> 41.8 us (0.977)
  Pallas kernels: 41 us -> 40 us
    pallas_call x1, Pallas kernels: 41 us -> 40 us  [on_device(): pl.pallas_call(functools.partial(kernel, nr, nc), out_shape=jax.ShapeDtyp...]
where the time goes in v4:
time: 41.8 us; the launch traced here: 41.6 us
  Pallas kernels  40 us (96%)
  local copies, waits for them, and re-layouts  1.57 us (4%)
    pallas_call x1, Pallas kernels, on_device(): pl.pallas_call(functools.partial(kernel, nr, nc), out_shape=jax.ShapeDtyp...  40 us
    unnamed x1, local copies, waits for them, and re-layouts  1.57 us

profile of v4, /device:TPU:0, one launch (start us, length us, event | category | flops | bytes accessed | tf_op | source)
XLA Modules:
  0.0 41.6 jit_solution(5476309649941435880)
XLA Ops:
  0.0 40.0 %shard_map.46 = f32[128,256]{1,0:T(8,128)} custom-call(bf16[1024,2048]{1,0:T(8,128)(2,1)} %resp.1, bf16[32,192]{1,0:T(8,128)(2,1)} %tm.1, bf16[64,2048]{1,0:T(8,128)(2,1)} %bitcast.1, s32[1,2]{1,0:T(1,128)} %ranks.1), custom_call_target="tpu_custom_call" | custom-call | tf_op jit(solution)/shard_map/pallas_call | solution.py:277
  40.0 1.6 %copy.6 = f32[128,256]{1,0:T(8,128)} copy(f32[128,256]{1,0:T(8,128)} %shard_map.46) | data formatting | bytes 262144
